TPU v7x, 32 devices: a whole 2x2x4 slice. The times are simulated.
32 devices in a mesh: dap: 8 (over y, x, core), seq: 4 (over z).
Axes of the slice: x: 2, y: 2, z: 4, core: 2. Of those that a mesh axis runs over, the one named last changes fastest.
Arguments:
- homolog_tensor: bfloat16 [8, 32, 256], P('dap', 'seq'), may hold values from -6 to 6
- pair_features: bfloat16 [32, 32, 128], P('seq', 'dap'), may hold values from -6 to 6
- entry_real_mask: int32 [8, 32], P('dap', 'seq'), may hold values 0 or 1
- chain_ids: int32 [32], replicated, may hold values from 0 to 3, never falling along the last dimension, each value on 1 to 16 neighbouring positions
- horizontal_matrices: bfloat16 [256, 1024], replicated, may hold values from -0.375 to 0.375
- horizontal_projector: bfloat16 [256, 256], replicated, may hold values from -0.375 to 0.375
- bias_proj: float32 [128, 8], replicated, may hold values from -35.35534 to 35.35534
- chain_bias: float32 [2, 8], replicated, may hold values from -4 to 4
- column_proj: bfloat16 [256, 1024], replicated, may hold values from -12.5 to 12.5
- vertical_projector: bfloat16 [256, 256], replicated, may hold values from -0.375 to 0.375
- expansion_matrix: bfloat16 [256, 1024], replicated, may hold values from -0.375 to 0.375
- contraction_matrix: bfloat16 [1024, 256], replicated, may hold values from -0.1875 to 0.1875
Outputs:
- updated: bfloat16 [8, 32, 256], P('dap', 'seq')
Inputs may be any that keep to these rules, and one draw needn't show every extreme that they name: `chain_ids`: chain numbers never fall along the residues.
All inputs are finite; a program needn't handle non-finite values. No bound on the sum of `entry_real_mask` on one device may be relied on, other than what follows from the above.
Results may differ from a plain program's by a relative error of at most 0.013.
The roundings to bfloat16 on the way count: a program that leaves them out, or rounds other values in their place, can miss the bound.
Values may be sent and summed in bfloat16 or wider, within the bound.
No kernel may reach another device: no remote copies, remote signals or barrier semaphores. Data moves between devices by JAX's collectives and lax.ppermute only.
A program may use at most 64 MiB of HBM per device.

v0:
```python
import jax
import jax.numpy as jnp
from jax import lax
from jax.sharding import PartitionSpec as P

HEAD_TOTAL = 8
HEAD_DEPTH = 32
epsilon = 1e-05


def layer_norm(inputs):
    center = inputs - jnp.mean(inputs, axis=-1, keepdims=True)
    spread = jnp.mean(center * center, axis=-1, keepdims=True)
    return center * lax.rsqrt(spread + epsilon)


def attend(queries, key_part, value_part, keep_mask, bias_term):
    scores = jnp.einsum(
        "ihd,jhd->hij", queries, key_part, preferred_element_type=jnp.float32
    ) * HEAD_DEPTH ** (-0.5)
    if bias_term is not None:
        scores = scores + bias_term.astype(jnp.float32)
    scores = jnp.where(keep_mask[None, None, :] > 0, scores, -1000000000.0)
    weights = jax.nn.softmax(scores, axis=-1).astype(jnp.bfloat16)
    return jnp.einsum("hij,jhd->ihd", weights, value_part, preferred_element_type=jnp.float32)


def column_update(
    column, keep_column, column_proj, vertical_projector, expansion_matrix, contraction_matrix
):
    expanded_dimension = HEAD_TOTAL * HEAD_DEPTH
    standardized = layer_norm(column.astype(jnp.float32)).astype(jnp.bfloat16)
    projected = jnp.dot(standardized, column_proj, preferred_element_type=jnp.float32).astype(
        jnp.bfloat16
    )
    queries = projected[:, :expanded_dimension].reshape(-1, HEAD_TOTAL, HEAD_DEPTH)
    key_part = projected[:, expanded_dimension : 2 * expanded_dimension].reshape(
        -1, HEAD_TOTAL, HEAD_DEPTH
    )
    value_part = projected[:, 2 * expanded_dimension : 3 * expanded_dimension].reshape(
        -1, HEAD_TOTAL, HEAD_DEPTH
    )
    attended = attend(queries, key_part, value_part, keep_column, None).reshape(
        -1, expanded_dimension
    )
    sigmoid_scaled = (
        jax.nn.sigmoid(projected[:, 3 * expanded_dimension :].astype(jnp.float32)) * attended
    ).astype(jnp.bfloat16)
    mixed = column.astype(jnp.float32) + jnp.dot(
        sigmoid_scaled, vertical_projector, preferred_element_type=jnp.float32
    )
    inner = jnp.maximum(
        jnp.dot(
            layer_norm(mixed).astype(jnp.bfloat16),
            expansion_matrix,
            preferred_element_type=jnp.float32,
        ),
        0.0,
    ).astype(jnp.bfloat16)
    return (mixed + jnp.dot(inner, contraction_matrix, preferred_element_type=jnp.float32)).astype(
        jnp.bfloat16
    )


def body(
    homolog_tensor,
    pair_features,
    entry_real_mask,
    chain_ids,
    horizontal_matrices,
    horizontal_projector,
    bias_proj,
    chain_bias,
    column_proj,
    vertical_projector,
    expansion_matrix,
    contraction_matrix,
):
    row_count, local_residues, channels = homolog_tensor.shape
    expanded_dimension = HEAD_TOTAL * HEAD_DEPTH
    dap_count = lax.axis_size("dap")
    pair_rows, pair_columns, pair_width = pair_features.shape
    normed_pair = layer_norm(pair_features.astype(jnp.float32))
    projected_pair = jnp.einsum(
        "ijc,ch->hij", normed_pair, bias_proj, precision=lax.Precision.HIGHEST
    )
    row_chain = lax.dynamic_slice_in_dim(chain_ids, lax.axis_index("seq") * pair_rows, pair_rows)
    column_chain = lax.dynamic_slice_in_dim(
        chain_ids, lax.axis_index("dap") * pair_columns, pair_columns
    )
    same_chain = (row_chain[:, None] == column_chain[None, :]).astype(jnp.float32)
    chain_term = chain_bias[0][:, None, None] * same_chain + chain_bias[1][:, None, None] * (
        1.0 - same_chain
    )
    local_bias = (projected_pair + chain_term).astype(jnp.bfloat16)
    pair_bias = lax.all_gather(local_bias, "dap", axis=2, tiled=True)
    standardized = layer_norm(homolog_tensor.astype(jnp.float32)).astype(jnp.bfloat16)
    flat = standardized.reshape(-1, channels)
    keep_mask = entry_real_mask.astype(jnp.bfloat16)
    projected = (
        jnp.dot(flat, horizontal_matrices, preferred_element_type=jnp.float32)
        .astype(jnp.bfloat16)
        .reshape(row_count, local_residues, 4 * expanded_dimension)
    )
    queries = projected[..., :expanded_dimension]
    gating = projected[..., 3 * expanded_dimension :]
    key_values, keep_all = (
        lax.all_gather(
            projected[..., expanded_dimension : 3 * expanded_dimension], "seq", axis=1, tiled=True
        ),
        lax.all_gather(keep_mask, "seq", axis=1, tiled=True),
    )

    def one_row(inputs_row):
        row_queries, row_pairs, row_keep = inputs_row
        key_part = row_pairs[:, :expanded_dimension].reshape(-1, HEAD_TOTAL, HEAD_DEPTH)
        value_part = row_pairs[:, expanded_dimension:].reshape(-1, HEAD_TOTAL, HEAD_DEPTH)
        return attend(
            row_queries.reshape(local_residues, HEAD_TOTAL, HEAD_DEPTH),
            key_part,
            value_part,
            row_keep,
            pair_bias,
        ).reshape(local_residues, expanded_dimension)

    attended = lax.map(one_row, (queries, key_values, keep_all))
    sigmoid_scaled = (jax.nn.sigmoid(gating.astype(jnp.float32)) * attended).astype(jnp.bfloat16)
    row_result = jnp.dot(
        sigmoid_scaled.reshape(-1, expanded_dimension),
        horizontal_projector,
        preferred_element_type=jnp.float32,
    ).reshape(row_count, local_residues, channels)
    updated_rows = (homolog_tensor.astype(jnp.float32) + row_result).astype(jnp.bfloat16)
    per_device = local_residues // dap_count
    blocks = updated_rows.reshape(row_count, dap_count, per_device, channels)
    keep_blocks = keep_mask.reshape(row_count, dap_count, per_device)

    def single_column(inputs_col):
        return column_update(
            inputs_col[0],
            inputs_col[1],
            column_proj,
            vertical_projector,
            expansion_matrix,
            contraction_matrix,
        )

    column_block = lax.all_to_all(blocks, "dap", split_axis=1, concat_axis=0, tiled=True)
    column_keep = lax.all_to_all(keep_blocks, "dap", split_axis=1, concat_axis=0, tiled=True)
    inputs_col = (jnp.moveaxis(column_block[:, 0], 1, 0), jnp.moveaxis(column_keep[:, 0], 1, 0))
    output_list = lax.map(single_column, inputs_col)
    mixed = jnp.moveaxis(output_list, 0, 1)[:, None]
    returned = lax.all_to_all(mixed, "dap", split_axis=0, concat_axis=1, tiled=True)
    return returned.reshape(row_count, local_residues, channels)


def solution(mesh):
    placed = (
        P("dap", "seq", None),
        P("seq", "dap", None),
        P("dap", "seq"),
        P(),
        P(),
        P(),
        P(),
        P(),
        P(),
        P(),
        P(),
        P(),
    )
    return jax.shard_map(
        body, mesh=mesh, in_specs=placed, out_specs=P("dap", "seq", None), check_vma=False
    )
```

profile of v0, /device:TPU:0, one launch (start us, length us, event | category | flops | bytes accessed | tf_op | source)
XLA Modules:
  0.0 71.7 jit_solution(17577258312015481253)
XLA Ops:
  0.0 0.7 convert_bitcast_fusion.1
  0.7 0.7 copy.49
  1.4 5.2 %all-to-all-start.1 = ((bf16[1,8,1]{2,0,1:T(2,128)(2,1)}), bf16[1,8,1]{2,0,1:T(2,128)(2,1)S(1)}, u32[]{:S(2)}, u32[]{:S(2)}) async-start(bf16[1,8,1]{2,0,1:T(2,128)(2,1)} %copy.49), calls=%async_computation.1 | async-start | bytes 8192 | tf_op jit(solution)/shard_map/all_to_all | solution.py:149
  6.6 0.7 copy-done.12
  7.6 0.5 copy-done.6
  8.6 0.6 copy-done.7
  9.2 0.7 copy-done.5
  10.2 0.6 copy-done.9
  10.8 0.7 copy-done.11
  11.7 9.7 %all_gather.11 = bf16[8,8,32]{1,0,2:T(8,128)(2,1)S(1)} all-gather(bf16[8,8,4]{1,0,2:T(8,128)(2,1)S(1)} %copy.43), channel_id=1, replica_groups=mesh['dap'=8,'seq'=4] {'dap'}, dimensions={2}, use_global_device_ids=true | all-gather | bytes 4608 | tf_op jit(solution)/shard_map/all_gather | solution.py:96
  21.6 0.6 slice-done
  22.2 13.4 %all_gather.9 = bf16[1,32,512]{2,1,0:T(8,128)(2,1)S(1)} all-gather(bf16[1,8,512]{2,1,0:T(8,128)(2,1)S(1)} %slice-done), channel_id=1, replica_groups=mesh['dap'=8,'seq'=4] {'seq'}, dimensions={1}, use_global_device_ids=true | all-gather | bytes 40960 | tf_op jit(solution)/shard_map/all_gather | solution.py:108
  35.7 0.6 slice-done.1
  36.3 0.6 dynamic-slice
  37.8 11.7 %all-reduce = bf16[32]{0:T(256)(128)(2,1)S(1)} all-reduce(bf16[32]{0:T(256)(128)(2,1)S(1)} %dynamic-update-slice), channel_id=1, replica_groups=mesh['dap'=8,'seq'=4] {'seq'}, use_global_device_ids=true, to_apply=%add | all-reduce | flops 32 | bytes 128
  50.3 0.5 copy-done.3
  51.2 0.6 broadcast.220
  51.8 0.7 %reduce.5 = bf16[8,256]{1,0:T(8,128)(2,1)S(1)} reduce(bf16[8,1,1,256]{3,2,1,0:T(2,128)(2,1)S(1)} %bitcast.75, bf16[]{:T(256)} %broadcast.220), dimensions={1,2}, to_apply=%bitcast.73.reduce_sub_computation | reduce | bytes 8194
  52.5 0.6 reshape.228
  53.1 3.3 %all-to-all-start = ((bf16[8,2,128]{2,1,0:T(2,128)(2,1)}), bf16[8,2,128]{2,1,0:T(2,128)(2,1)S(1)}, u32[]{:S(2)}, u32[]{:S(2)}) async-start(bf16[8,2,128]{2,1,0:T(2,128)(2,1)} %reshape.228), calls=%async_computation | async-start | bytes 8192 | tf_op jit(solution)/shard_map/all_to_all | solution.py:148
  56.6 4.3 %all-to-all-done = bf16[8,2,128]{2,1,0:T(2,128)(2,1)S(1)} async-done(((bf16[8,2,128]{2,1,0:T(2,128)(2,1)}), bf16[8,2,128]{2,1,0:T(2,128)(2,1)S(1)}, u32[]{:S(2)}, u32[]{:S(2)}) %all-to-all-start) | async-done | bytes 4128 | tf_op jit(solution)/shard_map/all_to_all | solution.py:148
  63.3 0.7 reduce.6
  64.0 7.1 %all_to_all.12 = bf16[8,2,128]{2,1,0:T(2,128)(2,1)S(1)} all-to-all(bf16[8,2,128]{2,1,0:T(2,128)(2,1)S(1)} %reshape.230), channel_id=1, replica_groups=mesh['dap'=8,'seq'=4] {'dap'}, dimensions={0} | all-to-all | bytes 8192 | tf_op jit(solution)/shard_map/all_to_all | solution.py:153
  71.1 0.6 copy.83
  (79 shorter events, 5.5 us)
Async XLA Ops:
  0.0 8.3 %copy-start = (bf16[256,1024]{1,0:T(8,128)(2,1)S(1)}, bf16[256,1024]{1,0:T(8,128)(2,1)}, u32[]{:S(2)}) copy-start(bf16[256,1024]{1,0:T(8,128)(2,1)} %param.16) | copy-start | bytes 1572868
  1.4 51.7 %all-to-all-start.1 = ((bf16[1,8,1]{2,0,1:T(2,128)(2,1)}), bf16[1,8,1]{2,0,1:T(2,128)(2,1)S(1)}, u32[]{:S(2)}, u32[]{:S(2)}) async-start(bf16[1,8,1]{2,0,1:T(2,128)(2,1)} %copy.49), calls=%async_computation.1 | async-start | bytes 8192 | tf_op jit(solution)/shard_map/all_to_all | solution.py:149
  6.6 0.7 copy-start.12
  7.3 0.7 copy-start.6
  8.6 0.6 copy-start.7
  9.2 0.7 copy-start.5
  10.1 0.7 copy-start.9
  10.8 0.7 copy-start.11
  21.5 0.7 slice-start
  35.5 0.8 %copy-start.13 = (u32[32]{0:T(128)S(1)}, u32[32]{0:T(128)}, u32[]{:S(2)}) copy-start(u32[32]{0:T(128)} %constant.98) | copy-start | bytes 388
  35.5 0.7 slice-start.1
  35.5 25.7 %copy-start.10 = (bf16[256,1024]{1,0:T(8,128)(2,1)S(1)}, bf16[256,1024]{1,0:T(8,128)(2,1)}, u32[]{:S(2)}) copy-start(bf16[256,1024]{1,0:T(8,128)(2,1)} %param.20) | copy-start | bytes 1572868
  50.0 0.9 %copy-start.3 = (bf16[256,256]{1,0:T(8,128)(2,1)S(1)}, bf16[256,256]{1,0:T(8,128)(2,1)}, u32[]{:S(2)}) copy-start(bf16[256,256]{1,0:T(8,128)(2,1)} %param.17) | copy-start | bytes 393220
  50.3 0.7 %copy-start.8 = (bf16[1,8,1024]{2,1,0:T(8,128)(2,1)S(1)}, bf16[1,8,1024]{2,1,0:T(8,128)(2,1)}, u32[]{:S(2)}) copy-start(bf16[1,8,1024]{2,1,0:T(8,128)(2,1)} %copy-done.7) | copy-start | bytes 49156
  53.1 7.9 %all-to-all-start = ((bf16[8,2,128]{2,1,0:T(2,128)(2,1)}), bf16[8,2,128]{2,1,0:T(2,128)(2,1)S(1)}, u32[]{:S(2)}, u32[]{:S(2)}) async-start(bf16[8,2,128]{2,1,0:T(2,128)(2,1)} %reshape.228), calls=%async_computation | async-start | bytes 8192 | tf_op jit(solution)/shard_map/all_to_all | solution.py:148
  61.3 1.1 %copy-start.4 = (bf16[256,256]{1,0:T(8,128)(2,1)S(1)}, bf16[256,256]{1,0:T(8,128)(2,1)}, u32[]{:S(2)}) copy-start(bf16[256,256]{1,0:T(8,128)(2,1)} %param.21) | copy-start | bytes 393220
  61.3 1.6 %copy-start.2 = (bf16[256,1024]{1,0:T(8,128)(2,1)S(1)}, bf16[256,1024]{1,0:T(8,128)(2,1)}, u32[]{:S(2)}) copy-start(bf16[256,1024]{1,0:T(8,128)(2,1)} %param.22) | copy-start | bytes 1572868
  61.5 1.3 %copy-start.1 = (bf16[1024,256]{1,0:T(8,128)(2,1)S(1)}, bf16[1024,256]{1,0:T(8,128)(2,1)}, u32[]{:S(2)}) copy-start(bf16[1024,256]{1,0:T(8,128)(2,1)} %param.23) | copy-start | bytes 1572868
where the time goes:
time: 72.2 us; the launch traced here: 71.7 us
  blocking collectives  41.9 us (58%)
  local copies, waits for them, and re-layouts  9.98 us (14%)
  starting transfers between devices  8.51 us (12%)
  waiting for transfers between devices  4.3 us (6%)
  other arithmetic  3.88 us (5%)
  matrix products  2.23 us (3%)
  between operations  0.87 us (1%)
    all_gather x1, blocking collectives, body(): lax.all_gather(projected[..., expanded_dimension:3 * expanded_dimension],...  13.4 us
    unnamed x1, blocking collectives  11.7 us
    all_gather x1, blocking collectives, body(): pair_bias = lax.all_gather(local_bias, 'dap', axis=2, tiled=True)  9.75 us
    all_to_all x1, blocking collectives, body(): lax.all_to_all(mixed, 'dap', split_axis=0, concat_axis=1, tiled=True)  7.05 us
    unnamed x37, local copies, waits for them, and re-layouts  7.04 us
    all_to_all x1, starting transfers between devices, body(): lax.all_to_all(keep_blocks, 'dap', split_axis=1, concat_axis=0, tiled=True)  5.2 us
    all_to_all x1, waiting for transfers between devices, body(): lax.all_to_all(blocks, 'dap', split_axis=1, concat_axis=0, tiled=True)  4.3 us
    all_to_all x1, starting transfers between devices, body(): lax.all_to_all(blocks, 'dap', split_axis=1, concat_axis=0, tiled=True)  3.31 us
  transfers between devices with their start and end apart: 2, of which 1 were waited for; matrix products, arithmetic and copies ran while one was open for 8% of the time, Pallas kernels for 0%

commit v1 on v0

--- a/solution.py
+++ b/solution.py
@@ -6,6 +6,19 @@
 HEAD_TOTAL = 8
 HEAD_DEPTH = 32
 epsilon = 1e-05
+
+
+def collect(x, axis, dim):
+    ways = lax.axis_size(axis)
+    up = [(d, (d + 1) % ways) for d in range(ways)]
+    down = [(d, (d - 1) % ways) for d in range(ways)]
+    earlier, later = ([x], [x])
+    for _ in range(ways // 2):
+        earlier.append(lax.ppermute(earlier[-1], axis, up))
+    for _ in range((ways - 1) // 2):
+        later.append(lax.ppermute(later[-1], axis, down))
+    line = jnp.concatenate([*earlier[::-1], *later[1:]], axis=dim)
+    return jnp.roll(line, (lax.axis_index(axis) - ways // 2) * x.shape[dim], axis=dim)
 
 
 def layer_norm(inputs):
@@ -105,9 +118,7 @@
     queries = projected[..., :expanded_dimension]
     gating = projected[..., 3 * expanded_dimension :]
     key_values, keep_all = (
-        lax.all_gather(
-            projected[..., expanded_dimension : 3 * expanded_dimension], "seq", axis=1, tiled=True
-        ),
+        collect(projected[..., expanded_dimension : 3 * expanded_dimension], "seq", 1),
         lax.all_gather(keep_mask, "seq", axis=1, tiled=True),
     )
 

time: 72.2 us -> 60.4 us (0.84)
  blocking collectives: 41.9 us -> 26.9 us
  starting transfers between devices: 8.51 us -> 12.6 us
  local copies, waits for them, and re-layouts: 9.98 us -> 8.95 us
    all_gather x1 -> x0, blocking collectives: 13.4 us -> none  [body(): lax.all_gather(projected[..., expanded_dimension:3 * expanded_dimension],...]
    ppermute x0 -> x3, starting transfers between devices: none -> 5.41 us  [the longest x2 3.32 us: collect(): earlier.append(lax.ppermute(earlier[-1], axis, up))]
    unnamed x1, blocking collectives: 11.7 us -> 10.1 us
    all_to_all x1, starting transfers between devices: 5.2 us -> 3.88 us  [body(): lax.all_to_all(keep_blocks, 'dap', split_axis=1, concat_axis=0, tiled=True)]
    reduce_sum x3, other arithmetic: 0.31 us -> 1.07 us  [layer_norm(): center = inputs - jnp.mean(inputs, axis=-1, keepdims=True)]
    unnamed x37 -> x46, local copies, waits for them, and re-layouts: 7.04 us -> 6.57 us
  transfers between devices with their start and end apart: 2 -> 5, of which waited for: 1 -> 1; matrix products, arithmetic and copies ran while one was open for 8% -> 10% of each run, Pallas kernels for 0% -> 0%
where the time goes in v1:
time: 60.4 us; the launch traced here: 59.9 us
  blocking collectives  26.9 us (45%)
  starting transfers between devices  12.6 us (21%)
  local copies, waits for them, and re-layouts  8.95 us (15%)
  waiting for transfers between devices  4.31 us (7%)
  other arithmetic  3.83 us (6%)
  matrix products  2.34 us (4%)
  between operations  0.93 us (2%)
    unnamed x1, blocking collectives  10.1 us
    all_gather x1, blocking collectives, body(): pair_bias = lax.all_gather(local_bias, 'dap', axis=2, tiled=True)  9.75 us
    all_to_all x1, blocking collectives, body(): lax.all_to_all(mixed, 'dap', split_axis=0, concat_axis=1, tiled=True)  7.05 us
    unnamed x46, local copies, waits for them, and re-layouts  6.57 us
    all_to_all x1, waiting for transfers between devices, body(): lax.all_to_all(blocks, 'dap', split_axis=1, concat_axis=0, tiled=True)  4.3 us
    all_to_all x1, starting transfers between devices, body(): lax.all_to_all(keep_blocks, 'dap', split_axis=1, concat_axis=0, tiled=True)  3.88 us
    ppermute x2, starting transfers between devices, collect(): earlier.append(lax.ppermute(earlier[-1], axis, up))  3.32 us
    all_to_all x1, starting transfers between devices, body(): lax.all_to_all(blocks, 'dap', split_axis=1, concat_axis=0, tiled=True)  3.31 us
  transfers between devices with their start and end apart: 5, of which 1 were waited for; matrix products, arithmetic and copies ran while one was open for 10% of the time, Pallas kernels for 0%

profile of v1, /device:TPU:0, one launch (start us, length us, event | category | flops | bytes accessed | tf_op | source)
XLA Modules:
  0.0 59.9 jit_solution(10465568497459434872)
XLA Ops:
  0.0 0.9 %convert_reduce_fusion.1 = f32[8]{0:T(128)S(1)} fusion(bf16[1,8,256]{2,1,0:T(8,128)(2,1)} %param.12), kind=kLoop, calls=%fused_computation.57 | loop fusion | flops 4088 | bytes 4128 | tf_op jit(solution)/shard_map/reduce_sum | solution.py:25
  1.3 3.1 %collective-permute-start = (bf16[1,8,512]{2,1,0:T(8,128)(2,1)S(1)}, bf16[1,8,512]{2,1,0:T(8,128)(2,1)S(1)}, u32[]{:S(2)}, u32[]{:S(2)}) collective-permute-start(bf16[1,8,512]{2,1,0:T(8,128)(2,1)S(1)} %slice.51), channel_id=1, source_target_pairs={{0,1},{1,2},{2,3},{3,0},{4,5},{5,6},{6,7},{7,4},{8,9},{9,10},{10,1... | collective-permute-start | bytes 24584 | tf_op jit(solution)/shard_map/ppermute | solution.py:17
  4.4 2.1 %collective-permute-start.2 = (bf16[1,8,512]{2,1,0:T(8,128)(2,1)S(1)}, bf16[1,8,512]{2,1,0:T(8,128)(2,1)S(1)}, u32[]{:S(2)}, u32[]{:S(2)}) collective-permute-start(bf16[1,8,512]{2,1,0:T(8,128)(2,1)S(1)} %slice.51), channel_id=1, source_target_pairs={{0,3},{1,0},{2,1},{3,2},{4,7},{5,4},{6,5},{7,6},{8,11},{9,8},{10,9... | collective-permute-start | bytes 24584 | tf_op jit(solution)/shard_map/ppermute | solution.py:19
  6.5 0.7 %copy.56 = bf16[1,8,1]{2,0,1:T(2,128)(2,1)} copy(bf16[1,8,1]{1,2,0:T(2,128)(2,1)S(1)} %get-tuple-element.46) | data formatting | bytes 32 | tf_op jit(solution)/shard_map/reshape | solution.py:147
  7.2 3.9 %all-to-all-start.1 = ((bf16[1,8,1]{2,0,1:T(2,128)(2,1)}), bf16[1,8,1]{2,0,1:T(2,128)(2,1)S(1)}, u32[]{:S(2)}, u32[]{:S(2)}) async-start(bf16[1,8,1]{2,0,1:T(2,128)(2,1)} %copy.56), calls=%async_computation.1 | async-start | bytes 8192 | tf_op jit(solution)/shard_map/all_to_all | solution.py:160
  11.1 0.7 %copy-done.13 = s32[32]{0:T(128)S(1)} copy-done((s32[32]{0:T(128)S(1)}, s32[32]{0:T(128)}, u32[]{:S(2)}) %copy-start.13) | copy-done | bytes 152
  12.3 0.6 %copy-done.9 = f32[2,8]{1,0:T(2,128)S(1)} copy-done((f32[2,8]{1,0:T(2,128)S(1)}, f32[2,8]{1,0:T(2,128)}, u32[]{:S(2)}) %copy-start.9) | copy-done | bytes 88
  12.9 0.7 %copy-done.11 = f32[128,8]{0,1:T(8,128)S(1)} copy-done((f32[128,8]{0,1:T(8,128)S(1)}, f32[128,8]{0,1:T(8,128)}, u32[]{:S(2)}) %copy-start.11) | copy-done | bytes 4120
  13.9 0.6 %copy-done.14 = u32[32]{0:T(128)S(1)} copy-done((u32[32]{0:T(128)S(1)}, u32[32]{0:T(128)}, u32[]{:S(2)}) %copy-start.14) | copy-done | bytes 152
  14.5 0.6 dynamic-slice
  16.0 10.1 %all-reduce = bf16[32]{0:T(256)(128)(2,1)S(1)} all-reduce(bf16[32]{0:T(256)(128)(2,1)S(1)} %dynamic-update-slice), channel_id=1, replica_groups=mesh['dap'=8,'seq'=4] {'seq'}, use_global_device_ids=true, to_apply=%add | all-reduce | flops 32 | bytes 128
  26.5 9.7 %all_gather.7 = bf16[8,8,32]{1,0,2:T(8,128)(2,1)S(1)} all-gather(bf16[8,8,4]{1,0,2:T(8,128)(2,1)S(1)} %copy.50), channel_id=1, replica_groups=mesh['dap'=8,'seq'=4] {'dap'}, dimensions={2}, use_global_device_ids=true | all-gather | bytes 4608 | tf_op jit(solution)/shard_map/all_gather | solution.py:109
  36.3 0.6 slice-done
  37.0 0.7 %copy-done.6 = bf16[1,8,1024]{2,1,0:T(8,128)(2,1)S(1)} copy-done((bf16[1,8,1024]{2,1,0:T(8,128)(2,1)S(1)}, bf16[1,8,1024]{2,1,0:T(8,128)(2,1)}, u32[]{:S(2)}) %copy-start.6) | copy-done | bytes 16408
  38.7 0.5 copy-done.3
  39.4 0.6 broadcast.221
  40.0 0.7 %reduce.5 = bf16[8,256]{1,0:T(8,128)(2,1)S(1)} reduce(bf16[8,1,1,256]{3,2,1,0:T(2,128)(2,1)S(1)} %bitcast.75, bf16[]{:T(256)} %broadcast.221), dimensions={1,2}, to_apply=%bitcast.74.reduce_sub_computation | reduce | bytes 8194
  40.7 0.6 %reshape.228 = bf16[8,2,128]{2,1,0:T(2,128)(2,1)} reshape(bf16[8,256]{1,0:T(8,128)(2,1)S(1)} %reduce.5) | data formatting | bytes 8192
  41.3 3.3 %all-to-all-start = ((bf16[8,2,128]{2,1,0:T(2,128)(2,1)}), bf16[8,2,128]{2,1,0:T(2,128)(2,1)S(1)}, u32[]{:S(2)}, u32[]{:S(2)}) async-start(bf16[8,2,128]{2,1,0:T(2,128)(2,1)} %reshape.228), calls=%async_computation | async-start | bytes 8192 | tf_op jit(solution)/shard_map/all_to_all | solution.py:159
  44.9 4.3 %all-to-all-done = bf16[8,2,128]{2,1,0:T(2,128)(2,1)S(1)} async-done(((bf16[8,2,128]{2,1,0:T(2,128)(2,1)}), bf16[8,2,128]{2,1,0:T(2,128)(2,1)S(1)}, u32[]{:S(2)}, u32[]{:S(2)}) %all-to-all-start) | async-done | bytes 4128 | tf_op jit(solution)/shard_map/all_to_all | solution.py:159
  51.1 0.4 fusion.18
  51.5 0.7 %reduce.6 = bf16[8,256]{1,0:T(8,128)(2,1)S(1)} reduce(bf16[8,1,1,256]{3,0,2,1:T(8,128)(2,1)S(1)} %fusion.18, bf16[]{:T(256)} %broadcast.221), dimensions={1,2}, to_apply=%copy.62.reduce_sub_computation | reduce | bytes 8194 | tf_op jit(solution)/shard_map/broadcast_in_dim;transpose | solution.py:163
  52.2 7.1 %all_to_all.12 = bf16[8,2,128]{2,1,0:T(2,128)(2,1)S(1)} all-to-all(bf16[8,2,128]{2,1,0:T(2,128)(2,1)S(1)} %reshape.230), channel_id=1, replica_groups=mesh['dap'=8,'seq'=4] {'dap'}, dimensions={0} | all-to-all | bytes 8192 | tf_op jit(solution)/shard_map/all_to_all | solution.py:164
  59.3 0.6 %copy.88 = bf16[8,1,1,256]{3,0,1,2:T(8,128)(2,1)} copy(bf16[8,1,1,256]{3,2,1,0:T(2,128)(2,1)S(1)} %reshape.231) | data formatting | bytes 8192
  (92 shorter events, 5.2 us)
Async XLA Ops:
  0.0 1.1 %copy-start = (bf16[256,1024]{1,0:T(8,128)(2,1)S(1)}, bf16[256,1024]{1,0:T(8,128)(2,1)}, u32[]{:S(2)}) copy-start(bf16[256,1024]{1,0:T(8,128)(2,1)} %param.16) | copy-start | bytes 1572868
  0.0 0.9 %copy-start.7 = (bf16[1,8,256]{2,1,0:T(8,128)(2,1)S(1)}, bf16[1,8,256]{2,1,0:T(8,128)(2,1)}, u32[]{:S(2)}) copy-start(bf16[1,8,256]{2,1,0:T(8,128)(2,1)} %param.12) | copy-start | bytes 12292
  1.3 25.1 %copy-start.5 = (bf16[1,8,1024]{2,1,0:T(8,128)(2,1)}, bf16[1,8,1024]{2,1,0:T(8,128)(2,1)S(1)}, u32[]{:S(2)}) copy-start(bf16[1,8,1024]{2,1,0:T(8,128)(2,1)S(1)} %fusion.12) | copy-start | bytes 49156
  1.3 5.2 %copy-start.12 = (s32[1,8]{1,0:T(1,128)S(1)}, s32[1,8]{1,0:T(1,128)}, u32[]{:S(2)}) copy-start(s32[1,8]{1,0:T(1,128)} %param.14) | copy-start | bytes 100
  1.3 24.8 %collective-permute-start = (bf16[1,8,512]{2,1,0:T(8,128)(2,1)S(1)}, bf16[1,8,512]{2,1,0:T(8,128)(2,1)S(1)}, u32[]{:S(2)}, u32[]{:S(2)}) collective-permute-start(bf16[1,8,512]{2,1,0:T(8,128)(2,1)S(1)} %slice.51), channel_id=1, source_target_pairs={{0,1},{1,2},{2,3},{3,0},{4,5},{5,6},{6,7},{7,4},{8,9},{9,10},{10,1... | collective-permute-start | bytes 24584 | tf_op jit(solution)/shard_map/ppermute | solution.py:17
  4.4 33.3 %collective-permute-start.2 = (bf16[1,8,512]{2,1,0:T(8,128)(2,1)S(1)}, bf16[1,8,512]{2,1,0:T(8,128)(2,1)S(1)}, u32[]{:S(2)}, u32[]{:S(2)}) collective-permute-start(bf16[1,8,512]{2,1,0:T(8,128)(2,1)S(1)} %slice.51), channel_id=1, source_target_pairs={{0,3},{1,0},{2,1},{3,2},{4,7},{5,4},{6,5},{7,6},{8,11},{9,8},{10,9... | collective-permute-start | bytes 24584 | tf_op jit(solution)/shard_map/ppermute | solution.py:19
  7.2 34.1 %all-to-all-start.1 = ((bf16[1,8,1]{2,0,1:T(2,128)(2,1)}), bf16[1,8,1]{2,0,1:T(2,128)(2,1)S(1)}, u32[]{:S(2)}, u32[]{:S(2)}) async-start(bf16[1,8,1]{2,0,1:T(2,128)(2,1)} %copy.56), calls=%async_computation.1 | async-start | bytes 8192 | tf_op jit(solution)/shard_map/all_to_all | solution.py:160
  11.1 0.8 %copy-start.8 = (bf16[8,4,128]{2,1,0:T(4,128)(2,1)S(1)}, bf16[8,4,128]{2,1,0:T(4,128)(2,1)}, u32[]{:S(2)}) copy-start(bf16[8,4,128]{2,1,0:T(4,128)(2,1)} %param.13) | copy-start | bytes 24580
  11.1 0.7 %copy-start.13 = (s32[32]{0:T(128)S(1)}, s32[32]{0:T(128)}, u32[]{:S(2)}) copy-start(s32[32]{0:T(128)} %param.15) | copy-start | bytes 388
  12.2 0.7 %copy-start.9 = (f32[2,8]{1,0:T(2,128)S(1)}, f32[2,8]{1,0:T(2,128)}, u32[]{:S(2)}) copy-start(f32[2,8]{1,0:T(2,128)} %param.19) | copy-start | bytes 196
  12.9 0.7 %copy-start.11 = (f32[128,8]{0,1:T(8,128)S(1)}, f32[128,8]{0,1:T(8,128)}, u32[]{:S(2)}) copy-start(f32[128,8]{0,1:T(8,128)} %param.18) | copy-start | bytes 12292
  13.8 0.7 %copy-start.14 = (u32[32]{0:T(128)S(1)}, u32[32]{0:T(128)}, u32[]{:S(2)}) copy-start(u32[32]{0:T(128)} %constant.121) | copy-start | bytes 388
  26.1 10.8 %collective-permute-start.1 = (bf16[1,8,512]{2,1,0:T(8,128)(2,1)S(1)}, bf16[1,8,512]{2,1,0:T(8,128)(2,1)S(1)}, u32[]{:S(2)}, u32[]{:S(2)}) collective-permute-start(bf16[1,8,512]{2,1,0:T(8,128)(2,1)S(1)} %collective-permute-done), channel_id=1, source_target_pairs={{0,1},{1,2},{2,3},{3,0},{4,5},{5,6},{6,7},{7,4},{8,9},{9,10},{10,1... | collective-permute-start | bytes 24584 | tf_op jit(solution)/shard_map/ppermute | solution.py:17
  36.2 0.7 %slice-start = ((bf16[1,8,1024]{2,1,0:T(8,128)(2,1)}), bf16[1,8,256]{2,1,0:T(8,128)(2,1)S(1)}, s32[]{:S(2)}) async-start(bf16[1,8,1024]{2,1,0:T(8,128)(2,1)} %copy-done.5), calls=%async_computation.3 | async-start | bytes 8192 | tf_op jit(solution)/shard_map/slice | solution.py:118
  37.0 0.7 %copy-start.6 = (bf16[1,8,1024]{2,1,0:T(8,128)(2,1)S(1)}, bf16[1,8,1024]{2,1,0:T(8,128)(2,1)}, u32[]{:S(2)}) copy-start(bf16[1,8,1024]{2,1,0:T(8,128)(2,1)} %copy-done.5) | copy-start | bytes 49156
  37.7 11.8 %copy-start.10 = (bf16[256,1024]{1,0:T(8,128)(2,1)S(1)}, bf16[256,1024]{1,0:T(8,128)(2,1)}, u32[]{:S(2)}) copy-start(bf16[256,1024]{1,0:T(8,128)(2,1)} %param.20) | copy-start | bytes 1572868
  38.3 0.9 %copy-start.3 = (bf16[256,256]{1,0:T(8,128)(2,1)S(1)}, bf16[256,256]{1,0:T(8,128)(2,1)}, u32[]{:S(2)}) copy-start(bf16[256,256]{1,0:T(8,128)(2,1)} %param.17) | copy-start | bytes 393220
  41.3 7.9 %all-to-all-start = ((bf16[8,2,128]{2,1,0:T(2,128)(2,1)}), bf16[8,2,128]{2,1,0:T(2,128)(2,1)S(1)}, u32[]{:S(2)}, u32[]{:S(2)}) async-start(bf16[8,2,128]{2,1,0:T(2,128)(2,1)} %reshape.228), calls=%async_computation | async-start | bytes 8192 | tf_op jit(solution)/shard_map/all_to_all | solution.py:159
  49.5 1.1 %copy-start.4 = (bf16[256,256]{1,0:T(8,128)(2,1)S(1)}, bf16[256,256]{1,0:T(8,128)(2,1)}, u32[]{:S(2)}) copy-start(bf16[256,256]{1,0:T(8,128)(2,1)} %param.21) | copy-start | bytes 393220
  49.5 1.6 %copy-start.2 = (bf16[256,1024]{1,0:T(8,128)(2,1)S(1)}, bf16[256,1024]{1,0:T(8,128)(2,1)}, u32[]{:S(2)}) copy-start(bf16[256,1024]{1,0:T(8,128)(2,1)} %param.22) | copy-start | bytes 1572868
  49.8 1.3 %copy-start.1 = (bf16[1024,256]{1,0:T(8,128)(2,1)S(1)}, bf16[1024,256]{1,0:T(8,128)(2,1)}, u32[]{:S(2)}) copy-start(bf16[1024,256]{1,0:T(8,128)(2,1)} %param.23) | copy-start | bytes 1572868
